TPU v7x, 32 devices: a whole 2x2x4 slice. The times are simulated.
32 devices in a mesh: dp: 4 (over y, x), expert: 8 (over z, core).
Axes of the slice: x: 2, y: 2, z: 4, core: 2. Of those that a mesh axis runs over, the one named last changes fastest.
Arguments:
- tokens: bfloat16 [4096, 1536], P(('dp', 'expert')), may hold values from -6 to 6
- grad_out: bfloat16 [4096, 1536], P(('dp', 'expert')), may hold values from -6 to 6
- expert_ids: int32 [4096, 4], P(('dp', 'expert')), may hold values from 0 to 7, all different within a row; in each aligned block of 128 rows (0 to 127, 128 to 255, ...) at most 96 rows name the same one
- gate_q: int32 [4096, 4], P(('dp', 'expert')), may hold values from 1 to 65535
- w_up: bfloat16 [8, 1536, 768], P('expert', 'dp'), may hold values from -0.15625 to 0.15625
- w_down: bfloat16 [8, 768, 1536], P('expert', None, 'dp'), may hold values from -0.21875 to 0.21875
Outputs:
- dw_up: bfloat16 [8, 1536, 768], P('expert', 'dp')
- dw_down: bfloat16 [8, 768, 1536], P('expert', None, 'dp')
Inputs may be any that keep to these rules, and one draw needn't show every extreme that they name: `expert_ids`: within the rows of one device no expert is named by more than 96 rows, a bound that some block reaches; the 4 ids of a row differ.
All inputs are finite; a program needn't handle non-finite values.
Results may differ from a plain program's by a relative error of at most 0.0064.
Values may be sent and summed in bfloat16 or wider, within the bound.
No kernel may reach another device: no remote copies, remote signals or barrier semaphores. Data moves between devices by JAX's collectives and lax.ppermute only.
A program may use at most 64 MiB of HBM per device.

v0:
```python
import jax
import jax.numpy as jnp
from jax import lax
from jax.sharding import PartitionSpec as P


def silu_slope(values):
    sigmoid_part = jax.nn.sigmoid(values)
    return sigmoid_part * (1.0 + values * (1.0 - sigmoid_part))


def summed_up(recv_rows, projected_grad):
    first_dims = (((0,), (0,)), ((), ()))
    partial_value = lax.dot_general(
        recv_rows, projected_grad, first_dims, preferred_element_type=jnp.float32
    ).astype(jnp.bfloat16)
    pieces = lax.all_to_all(partial_value[None], "dp", split_axis=1, concat_axis=0, tiled=True)
    return jnp.sum(pieces.astype(jnp.float32), axis=0, keepdims=True).astype(jnp.bfloat16)


def summed_down(activated, grad_rows):
    first_dims = (((0,), (0,)), ((), ()))
    partial_value = lax.dot_general(
        activated, grad_rows, first_dims, preferred_element_type=jnp.float32
    ).astype(jnp.bfloat16)
    pieces = lax.all_to_all(partial_value[None], "dp", split_axis=2, concat_axis=0, tiled=True)
    return jnp.sum(pieces.astype(jnp.float32), axis=0, keepdims=True).astype(jnp.bfloat16)


def shards(tokens, grad_out, expert_ids, gate_q, w_up, w_down):
    devices = lax.axis_size("expert")
    token_count, top_count = expert_ids.shape
    model_width = tokens.shape[1]
    capacity = max(2, token_count * top_count * 3 // (2 * devices))
    slot_expert = expert_ids.reshape(-1)
    onehot_table = (slot_expert[:, None] == jnp.arange(devices, dtype=jnp.int32)[None, :]).astype(
        jnp.int32
    )
    earlier = jnp.cumsum(onehot_table, axis=0) - onehot_table
    slot_rank = jnp.sum(earlier * onehot_table, axis=1)
    slot_target = slot_expert * capacity + slot_rank
    gate_values = gate_q.reshape(-1).astype(jnp.float32) * (1.0 / 65536.0)
    token_rows = jnp.repeat(tokens, top_count, axis=0)
    slot_grads = (
        gate_values[:, None] * jnp.repeat(grad_out, top_count, axis=0).astype(jnp.float32)
    ).astype(jnp.bfloat16)
    empty_rows = jnp.zeros((devices * capacity, model_width), jnp.bfloat16)
    send_tokens = empty_rows.at[slot_target].set(token_rows).reshape(devices, capacity, model_width)
    grad_slots = empty_rows.at[slot_target].set(slot_grads).reshape(devices, capacity, model_width)
    contract_last = (((1,), (1,)), ((), ()))
    up_whole = lax.all_gather(w_up, "dp", axis=1, tiled=True)[0]
    down_whole = lax.all_gather(w_down, "dp", axis=2, tiled=True)[0]
    recv_tokens = lax.all_to_all(send_tokens, "expert", split_axis=0, concat_axis=0, tiled=True)
    recv_rows = recv_tokens.reshape(-1, model_width)
    projected = jnp.dot(recv_rows, up_whole, preferred_element_type=jnp.float32)
    recv_grads = lax.all_to_all(grad_slots, "expert", split_axis=0, concat_axis=0, tiled=True)
    activated = jax.nn.silu(projected).astype(jnp.bfloat16)
    grad_rows = recv_grads.reshape(-1, model_width)
    act_grad = lax.dot_general(
        grad_rows, down_whole, contract_last, preferred_element_type=jnp.float32
    )
    projected_grad = (act_grad * silu_slope(projected)).astype(jnp.bfloat16)
    up_grad = summed_up(recv_rows, projected_grad)
    down_grad = summed_down(activated, grad_rows)
    return (up_grad, down_grad)


def solution(mesh):
    in_specs = (
        P(("dp", "expert"), None),
        P(("dp", "expert"), None),
        P(("dp", "expert"), None),
        P(("dp", "expert"), None),
        P("expert", "dp", None),
        P("expert", None, "dp"),
    )
    out_specs = (P("expert", "dp", None), P("expert", None, "dp"))
    return jax.shard_map(shards, mesh=mesh, in_specs=in_specs, out_specs=out_specs, check_vma=False)
```

profile of v0, /device:TPU:0, one launch (start us, length us, event | category | flops | bytes accessed | tf_op | source)
XLA Modules:
  0.0 307.0 jit_solution(6901323254794781142)
XLA Ops:
  12.4 4.7 %scatter_custom_fusion = bf16[768,1536]{1,0:T(8,128)(2,1)} fusion(s32[512]{0:T(512)S(1)} %bitcast.53, bf16[512,1536]{1,0:T(8,128)(2,1)S(1)} %reshape.112, bf16[]{:T(256)} %constant.7.clone.1), kind=kCustom, calls=%fused_computation.18 | custom fusion | bytes 2359298 | tf_op jit(solution)/shard_map/scatter | solution.py:48
  17.1 6.5 %all-to-all-start = ((bf16[8,96,1536]{2,1,0:T(8,128)(2,1)}), bf16[8,96,1536]{2,1,0:T(8,128)(2,1)}, u32[]{:S(2)}, u32[]{:S(2)}) async-start(bf16[8,96,1536]{2,1,0:T(8,128)(2,1)} %bitcast.4), calls=%async_computation | async-start | bytes 4718592 | tf_op jit(solution)/shard_map/all_to_all | solution.py:53
  24.7 2.3 convert_element_type.78
  27.2 6.0 %scatter_custom_fusion.1 = bf16[768,1536]{1,0:T(8,128)(2,1)} fusion(s32[512]{0:T(512)S(1)} %bitcast.54, f32[512,1536]{1,0:T(8,128)} %convert_element_type.78, f32[512]{0:T(512)S(1)} %mul.59, bf16[]{:T(256)} %constant.7.clone.1), kind=kCustom, calls=%fused_computation.14 | custom fusion | flops 1572864 | bytes 5507074 | tf_op jit(solution)/shard_map/scatter | solution.py:49
  33.3 45.1 %all-to-all-done = bf16[8,96,1536]{2,1,0:T(8,128)(2,1)} async-done(((bf16[8,96,1536]{2,1,0:T(8,128)(2,1)}), bf16[8,96,1536]{2,1,0:T(8,128)(2,1)}, u32[]{:S(2)}, u32[]{:S(2)}) %all-to-all-start) | async-done | bytes 2359328 | tf_op jit(solution)/shard_map/all_to_all | solution.py:53
  78.3 3.6 %all-to-all-start.1 = ((bf16[8,96,1536]{2,1,0:T(8,128)(2,1)}), bf16[8,96,1536]{2,1,0:T(8,128)(2,1)S(1)}, u32[]{:S(2)}, u32[]{:S(2)}) async-start(bf16[8,96,1536]{2,1,0:T(8,128)(2,1)} %bitcast.6), calls=%async_computation.1 | async-start | bytes 4718592 | tf_op jit(solution)/shard_map/all_to_all | solution.py:56
  82.7 5.8 %fusion.2 = f32[768,768]{1,0:T(8,128)} fusion(bf16[768,1536]{1,0:T(8,128)(2,1)} %bitcast.5, bf16[1,1536,768]{2,1,0:T(8,128)(2,1)} %all-gather.5.cloned.1.call-done), kind=kOutput, calls=%fused_computation.7 | convolution fusion | flops 1811939328 | bytes 7077888 | tf_op jit(solution)/shard_map/dot_general | solution.py:55
  88.5 34.7 %all-gather.3.cloned.1.call-done = bf16[1,768,1536]{2,1,0:T(8,128)(2,1)} async-done(((bf16[1,768,384]{2,1,0:T(8,128)(2,1)}), bf16[1,768,1536]{2,1,0:T(8,128)(2,1)}) %all-gather.3.cloned.1.call-update) | async-done | bytes 2359312 | tf_op jit(solution)/shard_map/all_gather | solution.py:52
  123.2 13.3 %all-to-all-done.1 = bf16[8,96,1536]{2,1,0:T(8,128)(2,1)S(1)} async-done(((bf16[8,96,1536]{2,1,0:T(8,128)(2,1)}), bf16[8,96,1536]{2,1,0:T(8,128)(2,1)S(1)}, u32[]{:S(2)}, u32[]{:S(2)}) %all-to-all-start.1) | async-done | bytes 2359328 | tf_op jit(solution)/shard_map/all_to_all | solution.py:56
  137.9 8.2 %fusion = bf16[1,1536,768]{2,1,0:T(8,128)(2,1)S(1)} fusion(bf16[768,1536]{1,0:T(8,128)(2,1)} %bitcast.5, f32[768,768]{1,0:T(8,128)} %fusion.2, bf16[768,1536]{1,0:T(8,128)(2,1)} %bitcast.48, bf16[1,768,1536]{2,1,0:T(8,128)(2,1)} %all-gather.3.cloned.1.call-done), kind=kOutput, calls=%fused_computation.5 | convolution fusion | flops 3630366720 | bytes 11796480 | tf_op jit(solution)/shard_map/dot_general | solution.py:14
  146.1 33.8 %copy.34 = bf16[1,1536,768]{2,0,1:T(2,128)(2,1)} copy(bf16[1,1536,768]{2,1,0:T(8,128)(2,1)S(1)} %fusion) | data formatting | bytes 4718592 | tf_op jit(solution)/shard_map/broadcast_in_dim | solution.py:17
  180.4 24.1 %reduce.7 = bf16[1536,768]{1,0:T(8,128)(2,1)S(1)} reduce(bf16[1536,1,768]{2,1,0:T(2,128)(2,1)} %bitcast.42, bf16[]{:T(256)} %broadcast.72), dimensions={1}, to_apply=%bitcast.41.reduce_sub_computation | reduce | bytes 4718594
  204.5 2.3 reshape.129
  206.8 3.9 %all-to-all-start.2 = ((bf16[4,2,147456]{2,1,0:T(2,128)(2,1)}), bf16[4,2,147456]{2,1,0:T(2,128)(2,1)S(1)}, u32[]{:S(2)}, u32[]{:S(2)}) async-start(bf16[4,2,147456]{2,1,0:T(2,128)(2,1)} %reshape.129), calls=%async_computation.2 | async-start | bytes 4718592 | tf_op jit(solution)/shard_map/all_to_all | solution.py:17
  210.6 5.9 %fusion.1 = bf16[1,768,1536]{2,1,0:T(8,128)(2,1)} fusion(bf16[768,1536]{1,0:T(8,128)(2,1)} %bitcast.49, f32[768,768]{1,0:T(8,128)} %fusion.2), kind=kOutput, calls=%fused_computation.6 | convolution fusion | flops 1816068096 | bytes 7077888 | tf_op jit(solution)/shard_map/dot_general | solution.py:23
  216.5 12.1 %copy.29 = bf16[1,768,1536]{1,0,2:T(2,128)(2,1)} copy(bf16[1,768,1536]{2,1,0:T(8,128)(2,1)} %fusion.1) | data formatting | bytes 4718592 | tf_op jit(solution)/shard_map/broadcast_in_dim | solution.py:26
  228.6 25.5 %reduce.8 = bf16[1536,768]{1,0:T(8,128)(2,1)} reduce(bf16[1536,1,768]{2,1,0:T(2,128)(2,1)} %bitcast.43, bf16[]{:T(256)} %broadcast.72), dimensions={1}, to_apply=%bitcast.34.reduce_sub_computation | reduce | bytes 4718594
  254.1 4.1 %reshape.131 = bf16[4,2,147456]{2,1,0:T(2,128)(2,1)} reshape(bf16[1536,768]{1,0:T(8,128)(2,1)} %reduce.8) | data formatting | bytes 4718592
  258.2 4.5 %all-to-all-start.3 = ((bf16[4,2,147456]{2,1,0:T(2,128)(2,1)}), bf16[4,2,147456]{2,1,0:T(2,128)(2,1)}, u32[]{:S(2)}, u32[]{:S(2)}) async-start(bf16[4,2,147456]{2,1,0:T(2,128)(2,1)} %reshape.131), calls=%async_computation.3 | async-start | bytes 4718592 | tf_op jit(solution)/shard_map/all_to_all | solution.py:26
  262.7 3.6 %reshape.130 = bf16[1536,1,768]{2,1,0:T(2,128)(2,1)} reshape(bf16[4,2,147456]{2,1,0:T(2,128)(2,1)S(1)} %all-to-all-done.2) | data formatting | bytes 4718592
  266.3 2.7 copy.31
  270.3 20.1 %all-to-all-done.3 = bf16[4,2,147456]{2,1,0:T(2,128)(2,1)} async-done(((bf16[4,2,147456]{2,1,0:T(2,128)(2,1)}), bf16[4,2,147456]{2,1,0:T(2,128)(2,1)}, u32[]{:S(2)}, u32[]{:S(2)}) %all-to-all-start.3) | async-done | bytes 2359328 | tf_op jit(solution)/shard_map/all_to_all | solution.py:26
  290.5 5.2 %reshape.132 = bf16[1536,1,768]{2,1,0:T(2,128)(2,1)} reshape(bf16[4,2,147456]{2,1,0:T(2,128)(2,1)} %all-to-all-done.3) | data formatting | bytes 4718592
  295.6 2.7 copy.32
  (35 shorter events, 12.3 us)
Async XLA Ops:
  17.1 7.2 %copy-start.1 = (bf16[128,1536]{1,0:T(8,128)(2,1)S(1)}, bf16[128,1536]{1,0:T(8,128)(2,1)}, u32[]{:S(2)}) copy-start(bf16[128,1536]{1,0:T(8,128)(2,1)} %param.7) | copy-start | bytes 1179652
  17.1 61.2 %all-to-all-start = ((bf16[8,96,1536]{2,1,0:T(8,128)(2,1)}), bf16[8,96,1536]{2,1,0:T(8,128)(2,1)}, u32[]{:S(2)}, u32[]{:S(2)}) async-start(bf16[8,96,1536]{2,1,0:T(8,128)(2,1)} %bitcast.4), calls=%async_computation | async-start | bytes 4718592 | tf_op jit(solution)/shard_map/all_to_all | solution.py:53
  23.6 59.2 %all-gather.5.cloned.1.call-start = ((), (), s32[]{:S(2)}) async-start(), calls=%async_computation.5 | async-start | bytes 2949120 | tf_op jit(solution)/shard_map/all_gather | solution.py:51
  24.7 2.3 copy-start.2
  78.3 58.2 %all-to-all-start.1 = ((bf16[8,96,1536]{2,1,0:T(8,128)(2,1)}), bf16[8,96,1536]{2,1,0:T(8,128)(2,1)S(1)}, u32[]{:S(2)}, u32[]{:S(2)}) async-start(bf16[8,96,1536]{2,1,0:T(8,128)(2,1)} %bitcast.6), calls=%async_computation.1 | async-start | bytes 4718592 | tf_op jit(solution)/shard_map/all_to_all | solution.py:56
  81.9 41.3 %all-gather.3.cloned.1.call-start = ((), (), s32[]{:S(2)}) async-start(), calls=%async_computation.4 | async-start | bytes 2949120 | tf_op jit(solution)/shard_map/all_gather | solution.py:52
  136.5 1.4 copy-start
  206.8 51.5 %all-to-all-start.2 = ((bf16[4,2,147456]{2,1,0:T(2,128)(2,1)}), bf16[4,2,147456]{2,1,0:T(2,128)(2,1)S(1)}, u32[]{:S(2)}, u32[]{:S(2)}) async-start(bf16[4,2,147456]{2,1,0:T(2,128)(2,1)} %reshape.129), calls=%async_computation.2 | async-start | bytes 4718592 | tf_op jit(solution)/shard_map/all_to_all | solution.py:17
  258.2 32.2 %all-to-all-start.3 = ((bf16[4,2,147456]{2,1,0:T(2,128)(2,1)}), bf16[4,2,147456]{2,1,0:T(2,128)(2,1)}, u32[]{:S(2)}, u32[]{:S(2)}) async-start(bf16[4,2,147456]{2,1,0:T(2,128)(2,1)} %reshape.131), calls=%async_computation.3 | async-start | bytes 4718592 | tf_op jit(solution)/shard_map/all_to_all | solution.py:26
Sparse Core Ops, SparseCore 0:
  26.2 38.7 all-gather.4
  84.6 38.5 all-gather.2
where the time goes:
time: 308 us; the launch traced here: 307 us
  waiting for transfers between devices  114 us (37%)
  local copies, waits for them, and re-layouts  80.2 us (26%)
  other arithmetic  59.7 us (19%)
  matrix products  19.9 us (6%)
  starting transfers between devices  18.7 us (6%)
  between operations  14.2 us (5%)
    unnamed x2, other arithmetic  49.6 us
    all_to_all x1, waiting for transfers between devices, shards(): lax.all_to_all(send_tokens, 'expert', split_axis=0, concat_axis=0, tiled=...  45.1 us
    all_gather x1, waiting for transfers between devices, shards(): down_whole = lax.all_gather(w_down, 'dp', axis=2, tiled=True)[0]  34.7 us
    broadcast_in_dim x1, local copies, waits for them, and re-layouts, summed_up(): partial_value[None]  33.8 us
    unnamed x15, local copies, waits for them, and re-layouts  24.3 us
    all_to_all x1, waiting for transfers between devices, summed_down(): lax.all_to_all(partial_value[None], 'dp', split_axis=2, concat_axis=0, ti...  20.1 us
    all_to_all x1, waiting for transfers between devices, shards(): lax.all_to_all(grad_slots, 'expert', split_axis=0, concat_axis=0, tiled=T...  13.3 us
    broadcast_in_dim x1, local copies, waits for them, and re-layouts, summed_down(): partial_value[None]  12.1 us
  transfers between devices with their start and end apart: 6, of which 4 were waited for; matrix products, arithmetic and copies ran while one was open for 23% of the time, Pallas kernels for 0%

commit v1 on v0

--- a/solution.py
+++ b/solution.py
@@ -49,7 +49,9 @@
     grad_slots = empty_rows.at[slot_target].set(slot_grads).reshape(devices, capacity, model_width)
     contract_last = (((1,), (1,)), ((), ()))
     up_whole = lax.all_gather(w_up, "dp", axis=1, tiled=True)[0]
-    down_whole = lax.all_gather(w_down, "dp", axis=2, tiled=True)[0]
+    down_whole = jnp.concatenate(
+        lax.all_to_all(jnp.stack([w_down] * lax.axis_size("dp")), "dp", 0, 0), axis=2
+    )[0]
     recv_tokens = lax.all_to_all(send_tokens, "expert", split_axis=0, concat_axis=0, tiled=True)
     recv_rows = recv_tokens.reshape(-1, model_width)
     projected = jnp.dot(recv_rows, up_whole, preferred_element_type=jnp.float32)

time: 308 us -> 334 us (1.084)
  waiting for transfers between devices: 114 us -> 135 us
  starting transfers between devices: 18.7 us -> 22.7 us
    all_gather x1, waiting for transfers between devices: 0.02 us -> 39.7 us  [shards(): up_whole = lax.all_gather(w_up, 'dp', axis=1, tiled=True)[0]]
    all_gather x1 -> x0, waiting for transfers between devices: 34.7 us -> none  [shards(): down_whole = lax.all_gather(w_down, 'dp', axis=2, tiled=True)[0]]
    all_to_all x0 -> x1, waiting for transfers between devices: none -> 21 us  [shards(): lax.all_to_all(jnp.stack([w_down] * lax.axis_size('dp')), 'dp', 0, 0)]
    all_to_all x0 -> x1, starting transfers between devices: none -> 5.32 us  [shards(): lax.all_to_all(jnp.stack([w_down] * lax.axis_size('dp')), 'dp', 0, 0)]
    all_to_all x1, waiting for transfers between devices: 13.3 us -> 8.33 us  [shards(): lax.all_to_all(grad_slots, 'expert', split_axis=0, concat_axis=0, tiled=T...]
    unnamed x15 -> x19, local copies, waits for them, and re-layouts: 24.3 us -> 23.8 us
  transfers between devices with their start and end apart: 6 -> 6, of which waited for: 4 -> 5; matrix products, arithmetic and copies ran while one was open for 23% -> 23% of each run, Pallas kernels for 0% -> 0%
where the time goes in v1:
time: 334 us; the launch traced here: 333 us
  waiting for transfers between devices  135 us (40%)
  local copies, waits for them, and re-layouts  81.5 us (24%)
  other arithmetic  59.1 us (18%)
  starting transfers between devices  22.7 us (7%)
  matrix products  19.8 us (6%)
  between operations  14.2 us (4%)
    unnamed x2, other arithmetic  49.7 us
    all_to_all x1, waiting for transfers between devices, shards(): lax.all_to_all(send_tokens, 'expert', split_axis=0, concat_axis=0, tiled=...  45.7 us
    all_gather x1, waiting for transfers between devices, shards(): up_whole = lax.all_gather(w_up, 'dp', axis=1, tiled=True)[0]  39.7 us
    broadcast_in_dim x1, local copies, waits for them, and re-layouts, summed_up(): partial_value[None]  33.8 us
    unnamed x19, local copies, waits for them, and re-layouts  23.8 us
    all_to_all x1, waiting for transfers between devices, shards(): lax.all_to_all(jnp.stack([w_down] * lax.axis_size('dp')), 'dp', 0, 0)  21 us
    all_to_all x1, waiting for transfers between devices, summed_down(): lax.all_to_all(partial_value[None], 'dp', split_axis=2, concat_axis=0, ti...  20 us
    broadcast_in_dim x1, local copies, waits for them, and re-layouts, summed_down(): partial_value[None]  12.1 us
  transfers between devices with their start and end apart: 6, of which 5 were waited for; matrix products, arithmetic and copies ran while one was open for 23% of the time, Pallas kernels for 0%

profile of v1, /device:TPU:0, one launch (start us, length us, event | category | flops | bytes accessed | tf_op | source)
XLA Modules:
  0.0 332.5 jit_solution(4464924576260747066)
XLA Ops:
  10.0 5.3 %all-to-all-start.2 = ((bf16[4,1,768,384]{2,3,1,0:T(8,128)(2,1)}), bf16[4,1,768,384]{2,3,1,0:T(8,128)(2,1)}, u32[]{:S(2)}, u32[]{:S(2)}) async-start(bf16[4,1,768,384]{2,3,1,0:T(8,128)(2,1)} %stack.2), calls=%async_computation.2 | async-start | bytes 4718592 | tf_op jit(solution)/shard_map/all_to_all | solution.py:53
  18.2 4.7 %scatter_custom_fusion = bf16[768,1536]{1,0:T(8,128)(2,1)} fusion(s32[512]{0:T(512)S(1)} %bitcast.54, bf16[512,1536]{1,0:T(8,128)(2,1)S(1)} %reshape.119, bf16[]{:T(256)} %constant.7.clone.1), kind=kCustom, calls=%fused_computation.16 | custom fusion | bytes 2359298 | tf_op jit(solution)/shard_map/scatter | solution.py:48
  23.0 21.0 %all-to-all-done.2 = bf16[4,1,768,384]{2,3,1,0:T(8,128)(2,1)} async-done(((bf16[4,1,768,384]{2,3,1,0:T(8,128)(2,1)}), bf16[4,1,768,384]{2,3,1,0:T(8,128)(2,1)}, u32[]{:S(2)}, u32[]{:S(2)}) %all-to-all-start.2) | async-done | bytes 2359328 | tf_op jit(solution)/shard_map/all_to_all | solution.py:53
  43.9 5.2 %all-to-all-start = ((bf16[8,96,1536]{2,1,0:T(8,128)(2,1)}), bf16[8,96,1536]{2,1,0:T(8,128)(2,1)}, u32[]{:S(2)}, u32[]{:S(2)}) async-start(bf16[8,96,1536]{2,1,0:T(8,128)(2,1)} %bitcast.4), calls=%async_computation | async-start | bytes 4718592 | tf_op jit(solution)/shard_map/all_to_all | solution.py:55
  52.1 6.1 %scatter_custom_fusion.1 = bf16[768,1536]{1,0:T(8,128)(2,1)} fusion(s32[512]{0:T(512)S(1)} %bitcast.55, f32[512,1536]{1,0:T(8,128)} %convert_element_type.78, f32[512]{0:T(512)S(1)} %mul.59, bf16[]{:T(256)} %constant.7.clone.1), kind=kCustom, calls=%fused_computation.12 | custom fusion | flops 1572864 | bytes 5507074 | tf_op jit(solution)/shard_map/scatter | solution.py:49
  58.2 45.7 %all-to-all-done = bf16[8,96,1536]{2,1,0:T(8,128)(2,1)} async-done(((bf16[8,96,1536]{2,1,0:T(8,128)(2,1)}), bf16[8,96,1536]{2,1,0:T(8,128)(2,1)}, u32[]{:S(2)}, u32[]{:S(2)}) %all-to-all-start) | async-done | bytes 2359328 | tf_op jit(solution)/shard_map/all_to_all | solution.py:55
  103.9 3.6 %all-to-all-start.1 = ((bf16[8,96,1536]{2,1,0:T(8,128)(2,1)}), bf16[8,96,1536]{2,1,0:T(8,128)(2,1)S(1)}, u32[]{:S(2)}, u32[]{:S(2)}) async-start(bf16[8,96,1536]{2,1,0:T(8,128)(2,1)} %bitcast.6), calls=%async_computation.1 | async-start | bytes 4718592 | tf_op jit(solution)/shard_map/all_to_all | solution.py:58
  108.3 39.7 %all-gather.2.cloned.1.call-done = bf16[1,1536,768]{2,1,0:T(8,128)(2,1)} async-done(((bf16[1,384,768]{2,1,0:T(8,128)(2,1)}), bf16[1,1536,768]{2,1,0:T(8,128)(2,1)}) %all-gather.2.cloned.1.call-update) | async-done | bytes 2359312 | tf_op jit(solution)/shard_map/all_gather | solution.py:51
  148.0 5.8 %fusion.2 = f32[768,768]{1,0:T(8,128)} fusion(bf16[768,1536]{1,0:T(8,128)(2,1)} %bitcast.5, bf16[1,1536,768]{2,1,0:T(8,128)(2,1)} %all-gather.2.cloned.1.call-done), kind=kOutput, calls=%fused_computation.7 | convolution fusion | flops 1811939328 | bytes 7077888 | tf_op jit(solution)/shard_map/dot_general | solution.py:57
  153.8 8.3 %all-to-all-done.1 = bf16[8,96,1536]{2,1,0:T(8,128)(2,1)S(1)} async-done(((bf16[8,96,1536]{2,1,0:T(8,128)(2,1)}), bf16[8,96,1536]{2,1,0:T(8,128)(2,1)S(1)}, u32[]{:S(2)}, u32[]{:S(2)}) %all-to-all-start.1) | async-done | bytes 2359328 | tf_op jit(solution)/shard_map/all_to_all | solution.py:58
  163.6 8.1 %fusion = bf16[1,1536,768]{2,1,0:T(8,128)(2,1)S(1)} fusion(bf16[768,1536]{1,0:T(8,128)(2,1)} %bitcast.5, f32[768,768]{1,0:T(8,128)} %fusion.2, bf16[768,1536]{1,0:T(8,128)(2,1)} %bitcast.48, bf16[768,1536]{0,1:T(8,128)(2,1)} %bitcast.11), kind=kOutput, calls=%fused_computation.5 | convolution fusion | flops 3630366720 | bytes 11796480 | tf_op jit(solution)/shard_map/dot_general | solution.py:14
  171.7 33.8 %copy.41 = bf16[1,1536,768]{2,0,1:T(2,128)(2,1)} copy(bf16[1,1536,768]{2,1,0:T(8,128)(2,1)S(1)} %fusion) | data formatting | bytes 4718592 | tf_op jit(solution)/shard_map/broadcast_in_dim | solution.py:17
  206.0 24.1 %reduce.7 = bf16[1536,768]{1,0:T(8,128)(2,1)S(1)} reduce(bf16[1536,1,768]{2,1,0:T(2,128)(2,1)} %bitcast.42, bf16[]{:T(256)} %broadcast.75), dimensions={1}, to_apply=%bitcast.41.reduce_sub_computation | reduce | bytes 4718594
  232.3 3.9 %all-to-all-start.3 = ((bf16[4,2,147456]{2,1,0:T(2,128)(2,1)}), bf16[4,2,147456]{2,1,0:T(2,128)(2,1)S(1)}, u32[]{:S(2)}, u32[]{:S(2)}) async-start(bf16[4,2,147456]{2,1,0:T(2,128)(2,1)} %reshape.136), calls=%async_computation.3 | async-start | bytes 4718592 | tf_op jit(solution)/shard_map/all_to_all | solution.py:17
  236.2 5.8 %fusion.1 = bf16[1,768,1536]{2,1,0:T(8,128)(2,1)} fusion(bf16[768,1536]{1,0:T(8,128)(2,1)} %bitcast.49, f32[768,768]{1,0:T(8,128)} %fusion.2), kind=kOutput, calls=%fused_computation.6 | convolution fusion | flops 1816068096 | bytes 7077888 | tf_op jit(solution)/shard_map/dot_general | solution.py:23
  242.0 12.1 %copy.36 = bf16[1,768,1536]{1,0,2:T(2,128)(2,1)} copy(bf16[1,768,1536]{2,1,0:T(8,128)(2,1)} %fusion.1) | data formatting | bytes 4718592 | tf_op jit(solution)/shard_map/broadcast_in_dim | solution.py:26
  254.1 25.5 %reduce.8 = bf16[1536,768]{1,0:T(8,128)(2,1)} reduce(bf16[1536,1,768]{2,1,0:T(2,128)(2,1)} %bitcast.43, bf16[]{:T(256)} %broadcast.75), dimensions={1}, to_apply=%bitcast.33.reduce_sub_computation | reduce | bytes 4718594
  279.6 4.1 %reshape.138 = bf16[4,2,147456]{2,1,0:T(2,128)(2,1)} reshape(bf16[1536,768]{1,0:T(8,128)(2,1)} %reduce.8) | data formatting | bytes 4718592
  283.7 4.5 %all-to-all-start.4 = ((bf16[4,2,147456]{2,1,0:T(2,128)(2,1)}), bf16[4,2,147456]{2,1,0:T(2,128)(2,1)}, u32[]{:S(2)}, u32[]{:S(2)}) async-start(bf16[4,2,147456]{2,1,0:T(2,128)(2,1)} %reshape.138), calls=%async_computation.4 | async-start | bytes 4718592 | tf_op jit(solution)/shard_map/all_to_all | solution.py:26
  288.2 3.7 %reshape.137 = bf16[1536,1,768]{2,1,0:T(2,128)(2,1)} reshape(bf16[4,2,147456]{2,1,0:T(2,128)(2,1)S(1)} %all-to-all-done.3) | data formatting | bytes 4718592
  291.9 2.7 copy.38
  295.9 20.0 %all-to-all-done.4 = bf16[4,2,147456]{2,1,0:T(2,128)(2,1)} async-done(((bf16[4,2,147456]{2,1,0:T(2,128)(2,1)}), bf16[4,2,147456]{2,1,0:T(2,128)(2,1)}, u32[]{:S(2)}, u32[]{:S(2)}) %all-to-all-start.4) | async-done | bytes 2359328 | tf_op jit(solution)/shard_map/all_to_all | solution.py:26
  315.9 5.2 %reshape.139 = bf16[1536,1,768]{2,1,0:T(2,128)(2,1)} reshape(bf16[4,2,147456]{2,1,0:T(2,128)(2,1)} %all-to-all-done.4) | data formatting | bytes 4718592
  321.2 2.7 copy.39
  (40 shorter events, 16.5 us)
Async XLA Ops:
  10.0 5.3 %copy-start.3 = (s32[128,4]{0,1:T(4,128)S(1)}, s32[128,4]{0,1:T(4,128)}, u32[]{:S(2)}) copy-start(s32[128,4]{0,1:T(4,128)} %param.8) | copy-start | bytes 6148
  10.0 7.3 %copy-start.2 = (bf16[128,1536]{1,0:T(8,128)(2,1)S(1)}, bf16[128,1536]{1,0:T(8,128)(2,1)}, u32[]{:S(2)}) copy-start(bf16[128,1536]{1,0:T(8,128)(2,1)} %param.6) | copy-start | bytes 1179652
  10.0 33.9 %all-to-all-start.2 = ((bf16[4,1,768,384]{2,3,1,0:T(8,128)(2,1)}), bf16[4,1,768,384]{2,3,1,0:T(8,128)(2,1)}, u32[]{:S(2)}, u32[]{:S(2)}) async-start(bf16[4,1,768,384]{2,3,1,0:T(8,128)(2,1)} %stack.2), calls=%async_computation.2 | async-start | bytes 4718592 | tf_op jit(solution)/shard_map/all_to_all | solution.py:53
  43.9 5.2 %copy-start.1 = (bf16[128,1536]{1,0:T(8,128)(2,1)S(1)}, bf16[128,1536]{1,0:T(8,128)(2,1)}, u32[]{:S(2)}) copy-start(bf16[128,1536]{1,0:T(8,128)(2,1)} %param.7) | copy-start | bytes 1179652
  43.9 60.0 %all-to-all-start = ((bf16[8,96,1536]{2,1,0:T(8,128)(2,1)}), bf16[8,96,1536]{2,1,0:T(8,128)(2,1)}, u32[]{:S(2)}, u32[]{:S(2)}) async-start(bf16[8,96,1536]{2,1,0:T(8,128)(2,1)} %bitcast.4), calls=%async_computation | async-start | bytes 4718592 | tf_op jit(solution)/shard_map/all_to_all | solution.py:55
  49.6 2.3 copy-start.4
  103.9 58.2 %all-to-all-start.1 = ((bf16[8,96,1536]{2,1,0:T(8,128)(2,1)}), bf16[8,96,1536]{2,1,0:T(8,128)(2,1)S(1)}, u32[]{:S(2)}, u32[]{:S(2)}) async-start(bf16[8,96,1536]{2,1,0:T(8,128)(2,1)} %bitcast.6), calls=%async_computation.1 | async-start | bytes 4718592 | tf_op jit(solution)/shard_map/all_to_all | solution.py:58
  107.5 40.4 %all-gather.2.cloned.1.call-start = ((), (), s32[]{:S(2)}) async-start(), calls=%async_computation.5 | async-start | bytes 2949120 | tf_op jit(solution)/shard_map/all_gather | solution.py:51
  162.1 1.5 copy-start
  232.3 51.4 %all-to-all-start.3 = ((bf16[4,2,147456]{2,1,0:T(2,128)(2,1)}), bf16[4,2,147456]{2,1,0:T(2,128)(2,1)S(1)}, u32[]{:S(2)}, u32[]{:S(2)}) async-start(bf16[4,2,147456]{2,1,0:T(2,128)(2,1)} %reshape.136), calls=%async_computation.3 | async-start | bytes 4718592 | tf_op jit(solution)/shard_map/all_to_all | solution.py:17
  283.7 32.2 %all-to-all-start.4 = ((bf16[4,2,147456]{2,1,0:T(2,128)(2,1)}), bf16[4,2,147456]{2,1,0:T(2,128)(2,1)}, u32[]{:S(2)}, u32[]{:S(2)}) async-start(bf16[4,2,147456]{2,1,0:T(2,128)(2,1)} %reshape.138), calls=%async_computation.4 | async-start | bytes 4718592 | tf_op jit(solution)/shard_map/all_to_all | solution.py:26
Sparse Core Ops, SparseCore 0:
  110.2 37.7 all-gather.1
